TPU v7x, 32 devices: a whole 2x2x4 slice. The times are simulated.
32 devices in a mesh: dp: 8 (over z, y), tensor: 4 (over x, core).
Axes of the slice: x: 2, y: 2, z: 4, core: 2. Of those that a mesh axis runs over, the one named last changes fastest.
Arguments:
- tokens: bfloat16 [8192, 768], P(('dp', 'tensor')), may hold values from -6 to 6
- cotangent: bfloat16 [8192, 768], P(('dp', 'tensor')), may hold values from -6 to 6
- segments: int32 [8192], P('dp'), may hold values from 0 to 95, as said below
- lengths: int32 [32, 2], P('dp'), may hold values from 2 to 197, as said below
- rel_index: int32 [8192, 256], P('dp'), may hold values from 0 to 731, as said below
- w_qkv: bfloat16 [2, 768, 3, 768], P(None, None, None, 'tensor'), may hold values from -0.21875 to 0.21875
- qv_bias: bfloat16 [2, 2, 768], P(None, None, 'tensor'), may hold values from -3 to 3
- w_out: bfloat16 [2, 768, 768], P(None, 'tensor'), may hold values from -0.875 to 0.875
- w_fc1: bfloat16 [2, 768, 3072], P(None, None, 'tensor'), may hold values from -0.21875 to 0.21875
- fc1_bias: bfloat16 [2, 3072], P(None, 'tensor'), may hold values from -3 to 3
- w_fc2: bfloat16 [2, 3072, 768], P(None, 'tensor'), may hold values from -0.109375 to 0.109375
- rel_table: bfloat16 [2, 732, 12], P(None, None, 'tensor'), may hold values from -5 to 5
- ln_gain: float32 [2, 2, 768], replicated, may hold values from 0.25 to 1.75
- ln_bias: float32 [2, 2, 768], replicated, may hold values from -2 to 2
- layer_scale: float32 [2, 2, 768], replicated, may hold values from 0.25 to 1.75
- row_bias: float32 [2, 2, 768], replicated, may hold values from -2 to 2
Outputs:
- result: bfloat16 [8192, 768], P(('dp', 'tensor'))
- d_tokens: float32 [8192, 768], P(('dp', 'tensor'))
- d_w_qkv: float32 [2, 768, 3, 768], P(None, None, None, 'tensor')
- d_qv_bias: float32 [2, 2, 768], P(None, None, 'tensor')
- d_w_out: float32 [2, 768, 768], P(None, 'tensor')
- d_w_fc1: float32 [2, 768, 3072], P(None, None, 'tensor')
- d_fc1_bias: float32 [2, 3072], P(None, 'tensor')
- d_w_fc2: float32 [2, 3072, 768], P(None, 'tensor')
- d_rel_table: float32 [2, 732, 12], P(None, None, 'tensor')
- d_ln_gain: float32 [2, 2, 768], replicated
- d_ln_bias: float32 [2, 2, 768], replicated
- d_layer_scale: float32 [2, 2, 768], replicated
- d_row_bias: float32 [2, 2, 768], replicated
Inputs may be any that keep to these rules, and one draw needn't show every extreme that they name: `segments`: rows with equal ids belong to one image, or to the padding that ends one bin of 256 rows. Bin b holds rows of id 3 b (its first image), then 3 b + 1 (its second image), then one or more rows of id 3 b + 2 (padding). `lengths`: the rows of a bin's first and second image, in the order of segments; an image of r by c patches has r c + 1 rows, its class token first, then its patches row by row; a bin's two lengths sum to 255 or less. `rel_index`: for rows i and j of one image: (dr + 13) * 27 + dc + 13 for two patches whose row and column offsets are dr and dc, 729 from the class token to a patch, 730 from a patch to the class token, 731 for the class token with itself. Other entries are arbitrary.
All inputs are finite; a program needn't handle non-finite values.
Results may differ from a plain program's by a relative error of at most 0.023.
Values may be sent and summed in bfloat16 or wider, within the bound.
A program may use at most 128 MiB of HBM per device.

v0:
```python
import functools
from typing import NamedTuple

import jax
import jax.numpy as jnp
from jax import lax
from jax.experimental import pallas as pl
from jax.experimental.pallas import tpu as pltpu
from jax.sharding import PartitionSpec as P

HEAD_DIM = 64
SIDE = 14
STRIDE = 2 * SIDE - 1
CELLS = SIDE * SIDE
CHUNK = 32
MESH = pl.DeviceIdType.MESH
BF16 = jnp.bfloat16
F32 = jnp.float32


def dot(left_side, right_side, left_axis=1, right_axis=0):
    return lax.dot_general(
        left_side,
        right_side,
        (((left_axis,), (right_axis,)), ((), ())),
        preferred_element_type=F32,
    )


class Group:
    def __init__(self, send_sems, recv_sems):
        own = lax.axis_index("tensor")
        self.core = own % 2
        self.near = own + 1 - 2 * self.core
        self.far = (own + 2) % 4
        self.far_chip = 1 - own // 2
        self.sems = (send_sems, recv_sems)

    def greet(self, barrier):
        for other in (self.near, self.far, self.far + 1 - 2 * self.core):
            pl.semaphore_signal(
                barrier, inc=1, device_id={"tensor": other}, device_id_type=MESH
            )
        return 3

    def copy(self, sent, arrived, source, target, other):
        return pltpu.make_async_remote_copy(
            src_ref=source,
            dst_ref=target,
            send_sem=self.sems[0].at[sent],
            recv_sem=self.sems[1].at[arrived],
            device_id={"tensor": other},
            device_id_type=MESH,
        )


class Exchange:
    COPIES = 10

    def __init__(self, group, base, gath, part, got, summed):
        self.group, self.base = group, base
        self.gath, self.part, self.got, self.summed = gath, part, got, summed
        self.rows = (part if gath is None else gath).shape[1] // 2
        self.keep = group.core * self.rows
        self.give = (1 - group.core) * self.rows

    def slot(self, stage):
        core = self.group.core
        return 2 + core + stage * (1 - 2 * core)

    def span(self, first):
        return pl.ds(pl.multiple_of(first, self.rows), self.rows)

    def symmetric(self, number, source, target, other):
        at = self.base + number
        return self.group.copy(at, at, source, target, other)

    def to_near(self):
        return self.symmetric(0, self.gath.at[0], self.gath.at[1], self.group.near)

    def across(self, stage):
        core, rows = self.group.core, self.span(self.keep)
        source = core + stage * (1 - 2 * core)
        return self.symmetric(
            2 + stage,
            self.gath.at[source, rows],
            self.gath.at[self.slot(stage), rows],
            self.group.far,
        )

    def relay(self, stage):
        rows = self.span(self.keep)
        return self.symmetric(
            4 + stage,
            self.gath.at[self.slot(stage), rows],
            self.gath.at[self.slot(1 - stage), rows],
            self.group.near,
        )

    def sum_near(self):
        return self.symmetric(1, self.part.at[1], self.got.at[0], self.group.near)

    def pair(self, stage):
        return self.symmetric(
            6 + stage,
            self.part.at[self.slot(stage), self.span(self.give)],
            self.got.at[1, self.span(stage * self.rows)],
            self.group.near,
        )

    def home(self, stage, sender):
        return self.group.copy(
            self.base + 8 + stage,
            self.base + 8 + sender,
            self.summed.at[self.span(stage * self.rows)],
            self.got.at[2, self.span(sender * self.rows)],
            self.group.far_chip * 2 + stage,
        )

    def start(self):
        self.to_near().start()

        @pl.when(self.group.core == 0)
        def _():
            self.across(0).start()

    def spread(self):
        self.to_near().wait_recv()

        @pl.when(self.group.core == 1)
        def _():
            self.across(0).start()

        self.across(1).start()

    def pass_on(self, stage):
        self.across(stage).wait_recv()
        self.relay(stage).start()

    def arrived(self, stage):
        self.relay(stage).wait_recv()

    def send_sum(self, stage):
        self.pair(stage).wait_recv()
        rows = self.span(stage * self.rows)
        self.summed[rows] = self.part[self.slot(stage), self.span(self.keep)] + self.got[1, rows]
        self.home(stage, self.group.core).start()

    def finish(self):
        self.sum_near().wait_recv()
        for sender in range(2):
            self.home(0, sender).wait_recv()

    def drain_gather(self):
        self.to_near().wait_send()
        for stage in range(2):
            self.across(stage).wait_send()
            self.relay(stage).wait_send()

    def drain_sum(self):
        self.sum_near().wait_send()
        for stage in range(2):
            self.pair(stage).wait_send()
            self.home(stage, self.group.core).wait_send()


def by_chunk(total_rows, body, size=CHUNK):
    def step(at, carry):
        return body(pl.ds(pl.multiple_of(at * size, size), size), carry)

    return step, total_rows // size


def norm_chunk(values, gain, shift):
    center = values - jnp.mean(values, -1, keepdims=True)
    inverse = lax.rsqrt(jnp.mean(center * center, -1, keepdims=True) + 1e-06)
    normal = center * inverse
    return (normal * gain + shift).astype(BF16), normal, inverse


def gelu_parts(values):
    share = 0.5 * (1.0 + lax.erf(values * 0.7071067811865476))
    slope = share + values * (jnp.exp(-0.5 * values * values) * 0.3989422804014327)
    return values * share, slope


SPAN = 384
LAST = (SIDE - 1) * (STRIDE + 1)
CLASS = LAST + 1
TABLE_WIDTH = 2 * SPAN


def prepare(head_count, lengths, index_rows, table, bias, spots, turned, same):
    rows = bias.shape[3]
    own = lax.axis_index("tensor")
    order = (own, own + 1 - 2 * (own % 2), (own + 2) % 4, 3 - own)

    ones = []
    for slot in range(4):
        first = lengths[order[slot], 0]
        both = first + lengths[order[slot], 1]

        def pick(row):
            return index_rows[pl.ds(order[slot] * rows + row, 1), :]

        at = lax.broadcasted_iota(jnp.int32, (1, rows), 1)
        code = LAST - jnp.where(at < first, pick(1), pick(first + 1))
        code = jnp.where((at == 0) | (at == first), CLASS, code)
        code = jnp.where(at < both, code, -1)
        upright = lax.broadcasted_iota(jnp.int32, (SPAN, rows), 0)
        spots[slot] = (upright == code).astype(F32).astype(BF16)
        column = jnp.transpose(jnp.broadcast_to(code.astype(F32), (128, rows)))
        column = jnp.concatenate([column] * (SPAN // 128), -1)
        flat = lax.broadcasted_iota(jnp.int32, (rows, SPAN), 1).astype(F32)
        ones.append((flat == column).astype(F32).astype(BF16))
        mirrored = jnp.where(column < CLASS, LAST - column, column)
        mirrored = jnp.where(column < 0, -1.0, mirrored)
        turned[slot] = (flat == mirrored).astype(F32).astype(BF16)

        def image_of(values):
            return (values >= first).astype(jnp.int32) + (values >= both).astype(jnp.int32)

        by_row = image_of(lax.broadcasted_iota(jnp.int32, (rows, rows), 0))
        by_col = image_of(lax.broadcasted_iota(jnp.int32, (rows, rows), 1))
        same[slot] = (by_row == by_col).astype(F32)

    key_at = lax.broadcasted_iota(jnp.int32, (SPAN, SPAN), 0)
    query_at = lax.broadcasted_iota(jnp.int32, (SPAN, SPAN), 1)
    shift = SPAN - LAST

    def each(at, carry):
        row = table[pl.ds(at, 1), :]
        rolled = pltpu.roll(
            jnp.broadcast_to(row, (SPAN, TABLE_WIDTH)), 0, 1, stride=1, stride_axis=0
        )
        pairs = rolled[:, SPAN:]
        tail = shift + STRIDE * STRIDE
        pairs = jnp.where(query_at == CLASS, row[:, tail : tail + 1], pairs)
        pairs = jnp.where(key_at == CLASS, row[:, tail + 1 : tail + 2], pairs)
        pairs = jnp.where(
            (query_at == CLASS) & (key_at == CLASS), row[:, tail + 2 : tail + 3], pairs
        ).astype(BF16)
        for slot in range(4):
            half = dot(ones[slot], pairs, 1, 1).astype(BF16)
            looked = dot(half, spots[slot])
            bias[at // head_count, slot, at % head_count] = jnp.where(
                same[slot] > 0.5, looked, -1000000000.0
            ).astype(BF16)
        return carry

    lax.fori_loop(0, table.shape[0], each, 0)


def shifted_table(rel_table):
    layers, entries, head_count = rel_table.shape
    shift = SPAN - LAST
    table = jnp.transpose(rel_table, (0, 2, 1)).reshape(layers * head_count, entries).astype(F32)
    return jnp.pad(table, ((0, 0), (shift, TABLE_WIDTH - shift - entries)))


def table_row(pairs):
    query_at = lax.broadcasted_iota(jnp.int32, (SPAN, SPAN), 0)
    key_at = lax.broadcasted_iota(jnp.int32, (SPAN, SPAN), 1)
    zero = jnp.zeros((SPAN, SPAN), F32)
    patches = jnp.where((query_at <= LAST) & (key_at <= LAST), pairs, zero)
    rolled = pltpu.roll(
        jnp.concatenate([patches, zero], -1), 0, 1, stride=1, stride_axis=0
    )
    row = jnp.sum(rolled, 0, keepdims=True)
    at = lax.broadcasted_iota(jnp.int32, (1, TABLE_WIDTH), 1)
    tails = (
        (query_at == CLASS) & (key_at <= LAST),
        (query_at <= LAST) & (key_at == CLASS),
        (query_at == CLASS) & (key_at == CLASS),
    )
    for number, mask in enumerate(tails):
        row = jnp.where(at == STRIDE * STRIDE + number, jnp.sum(jnp.where(mask, pairs, zero)), row)
    return row


class Names:
    def __init__(self, names, refs):
        for name, ref in zip(names, refs, strict=True):
            setattr(self, name, ref)


def load_all(pairs, sems):
    steps = []
    for place, (source, target) in enumerate(pairs):
        step = pltpu.make_async_copy(source, target, sems.at[place])
        step.start()
        steps.append(step)
    return steps


def each_chunk(rows, body):
    def step(at, carry):
        body(pl.ds(pl.multiple_of(at * CHUNK, CHUNK), CHUNK))
        return carry

    lax.fori_loop(0, rows // CHUNK, step, 0)


def attend_rows(refs, at, slot, first, head_count):
    qkv = refs.qkv
    rows = qkv.shape[2] // 2
    wide = qkv.shape[3] // 3
    span = pl.ds(first, rows)
    heads = []
    for head in range(head_count):
        lanes = slice(head * HEAD_DIM, (head + 1) * HEAD_DIM)
        queries = qkv[at, slot, span, 0:wide][:, lanes]
        keys = qkv[at, slot, :, wide : 2 * wide][:, lanes]
        values = qkv[at, slot, :, 2 * wide : 3 * wide][:, lanes]
        scores = dot(queries, keys, 1, 1) + refs.bias[at, slot, head, span].astype(F32)
        powers = jnp.exp(scores - jnp.max(scores, -1, keepdims=True))
        weights = (powers / jnp.sum(powers, -1, keepdims=True)).astype(BF16)
        refs.weights[at, slot, head, span] = weights
        heads.append(dot(weights, values).astype(BF16))
    heads.append(jnp.zeros((rows, wide - head_count * HEAD_DIM), BF16))
    refs.mixture[at, slot, span] = jnp.concatenate(heads, -1)


class ForwardInputs(NamedTuple):
    lengths: object
    tokens: object
    cotangent: object
    qv_bias: object
    fc1_bias: object
    table: object
    ln_gain: object
    ln_bias: object
    layer_scale: object
    row_bias: object
    index_in: object
    w_qkv_in: object
    w_out_in: object
    w_up_in: object
    w_down_in: object


class ForwardKept(NamedTuple):
    gath_a: object
    qkv: object
    weights: object
    mixture: object
    gath_b: object
    slope: object
    active: object


class ForwardOutputs(NamedTuple):
    gath_z_out: object
    spots: object
    turned: object
    grad: object
    normal_a: object
    normal_b: object
    inverse: object
    branch_a: object
    branch_b: object
    stream: object


class ForwardScratch(NamedTuple):
    gath_z: object
    bias: object
    same: object
    index_rows: object
    w_qkv: object
    w_out: object
    w_up: object
    w_down: object
    qkv_bias: object
    up_bias: object
    hidden: object
    part: object
    got: object
    summed: object
    own: object
    send_sems: object
    recv_sems: object
    load_sems: object
    out_sems: object


def forward_body(layers, head_count, *all_refs):
    kept_outs = tuple(name + "_kept" for name in ForwardKept._fields)
    refs = Names(
        (*ForwardInputs._fields, *kept_outs, *ForwardOutputs._fields, *ForwardKept._fields, *ForwardScratch._fields), all_refs
    )
    stream, own, got, part = refs.stream, refs.own, refs.got, refs.part
    rows, width = stream.shape
    half = rows // 2
    last = layers - 1
    used = refs.w_out_in.shape[1]
    wide = refs.w_out.shape[1]
    loads = load_all(
        (
            (refs.index_in, refs.index_rows),
            (refs.w_qkv_in, refs.w_qkv),
            *(
                (refs.w_out_in.at[at], refs.w_out.at[at, pl.ds(0, used)])
                for at in range(layers)
            ),
            (refs.w_up_in, refs.w_up),
            (refs.w_down_in, refs.w_down),
        ),
        refs.load_sems,
    )
    group = Group(refs.send_sems, refs.recv_sems)
    barrier = pltpu.get_barrier_semaphore()
    greeted = group.greet(barrier)
    pl.semaphore_wait(barrier, greeted)
    early = Exchange(group, 2 * Exchange.COPIES, refs.gath_z, None, None, None)

    def load(span):
        stream[span] = refs.tokens[span].astype(F32)

    each_chunk(rows, load)
    refs.qkv_bias[...] = jnp.zeros_like(refs.qkv_bias)
    for at in range(layers):
        refs.w_out[at, used:] = jnp.zeros_like(refs.w_out[at, used:])
        refs.up_bias[at] = refs.fc1_bias[at : at + 1].astype(F32)
        for half_at in range(2):
            first = 2 * half_at * wide
            refs.qkv_bias[at, :, first : first + used] = refs.qv_bias[
                at, half_at : half_at + 1
            ].astype(F32)

    def keep(number, at):
        source = getattr(refs, ForwardKept._fields[number])
        target = getattr(refs, kept_outs[number])
        return pltpu.make_async_copy(source.at[at], target.at[at], refs.out_sems.at[number, at])

    def layer(at, carry):
        trade = Exchange(group, 0, refs.gath_a.at[at], part, got, refs.summed)

        def enter(span):
            low, normal, inv = norm_chunk(
                stream[span], refs.ln_gain[at, 0:1], refs.ln_bias[at, 0:1]
            )
            refs.gath_a[at, 0, span] = low
            refs.normal_a[at, span] = normal
            refs.inverse[at, 0, span] = jnp.broadcast_to(inv, (CHUNK, 128))

        each_chunk(rows, enter)
        trade.start()

        @pl.when(at == 0)
        def _():
            place = lax.axis_index("tensor")
            length = refs.lengths[place, 0] + refs.lengths[place, 1]

            def mask(number, carry):
                span = pl.ds(pl.multiple_of(number * CHUNK, CHUNK), CHUNK)
                row = number * CHUNK + lax.broadcasted_iota(jnp.int32, (CHUNK, width), 0)
                values = jnp.where(row < length, refs.cotangent[span].astype(F32), 0.0)
                refs.grad[span] = values
                refs.gath_z[0, span] = (values * refs.layer_scale[last, 1:2]).astype(BF16)
                return carry

            lax.fori_loop(0, rows // CHUNK, mask, 0)

        trade.spread()

        @pl.when(at == 0)
        def _():
            early.start()
            early.spread()
            loads[0].wait()
            prepare(
                head_count,
                refs.lengths,
                refs.index_rows,
                refs.table,
                refs.bias,
                refs.spots,
                refs.turned,
                refs.same,
            )
            for step in loads[1:]:
                step.wait()

        scale = jnp.concatenate(
            [
                jnp.full((1, refs.qkv.shape[3] // 3), HEAD_DIM**-0.5, F32),
                jnp.full((1, 2 * refs.qkv.shape[3] // 3), 1.0, F32),
            ],
            -1,
        )

        def project(slot):
            mixed = dot(refs.gath_a[at, slot], refs.w_qkv[at])
            mixed = (mixed + refs.qkv_bias[at]).astype(BF16).astype(F32) * scale
            refs.qkv[at, slot] = mixed.astype(BF16)

        def attend(slot, first):
            attend_rows(refs, at, slot, first, head_count)
            return dot(refs.mixture[at, slot, pl.ds(first, half)], refs.w_out[at])

        def chip_slot(slot, carry):
            project(slot)

            def one(place, carry):
                first = pl.multiple_of(place * half, half)
                result = attend(slot, first)

                @pl.when(slot == 0)
                def _():
                    own[pl.ds(first, half)] = result

                @pl.when(slot == 1)
                def _():
                    part[1, pl.ds(first, half)] = result.astype(BF16)

                return carry

            lax.fori_loop(0, 2, one, 0)
            return carry

        lax.fori_loop(0, 2, chip_slot, 0)
        trade.sum_near().start()
        trade.pass_on(0)

        def far_slot(stage, carry):
            slot = trade.slot(stage)
            trade.arrived(stage)
            project(slot)

            def one(place, carry):
                first = pl.multiple_of(
                    place * trade.keep + (1 - place) * trade.give, half
                )
                part[slot, pl.ds(first, half)] = attend(slot, first).astype(BF16)

                @pl.when(place == 0)
                def _():
                    trade.pair(stage).start()

                return carry

            lax.fori_loop(0, 2, one, 0)
            trade.send_sum(stage)

            @pl.when(stage == 0)
            def _():
                trade.pass_on(1)

            return carry

        lax.fori_loop(0, 2, far_slot, 0)
        for number in range(4):
            keep(number, at).start()

        @pl.when(at == 0)
        def _():
            for stage in range(2):
                early.pass_on(stage)

        trade.finish()

        def between(span):
            total = own[span] + got[0, span].astype(F32) + got[2, span].astype(F32)
            branch = total + refs.row_bias[at, 0:1]
            refs.branch_a[at, span] = branch
            middle = stream[span] + refs.layer_scale[at, 0:1] * branch
            stream[span] = middle
            low, normal, inv = norm_chunk(middle, refs.ln_gain[at, 1:2], refs.ln_bias[at, 1:2])
            refs.gath_b[at, 0, span] = low
            refs.normal_b[at, span] = normal
            refs.inverse[at, 1, span] = jnp.broadcast_to(inv, (CHUNK, 128))

        each_chunk(rows, between)

        @pl.when(at < last)
        def _():
            trade_b = Exchange(
                group, Exchange.COPIES, refs.gath_b.at[at], part, got, refs.summed
            )
            trade_b.start()
            trade.drain_gather()
            trade.drain_sum()
            trade_b.spread()

            def raise_rows(slot):
                refs.hidden[...] = dot(refs.gath_b[at, slot], refs.w_up[at]) + refs.up_bias[at]

                def act(place, carry):
                    span = pl.ds(pl.multiple_of(place * 16, 16), 16)
                    high, incline = gelu_parts(refs.hidden[span])
                    refs.active[at, slot, span] = high.astype(BF16)
                    refs.slope[at, slot, span] = incline.astype(BF16)
                    return carry

                lax.fori_loop(0, rows // 16, act, 0)

            def lower(slot, first, count):
                return dot(refs.active[at, slot, pl.ds(first, count)], refs.w_down[at])

            def chip_slot(slot, carry):
                raise_rows(slot)
                result = lower(slot, 0, rows)

                @pl.when(slot == 0)
                def _():
                    own[...] = result

                @pl.when(slot == 1)
                def _():
                    part[1] = result.astype(BF16)

                return carry

            lax.fori_loop(0, 2, chip_slot, 0)
            trade_b.sum_near().start()
            trade_b.pass_on(0)

            def far_slot(stage, carry):
                slot = trade_b.slot(stage)
                trade_b.arrived(stage)
                raise_rows(slot)

                def one(place, carry):
                    first = pl.multiple_of(
                        place * trade_b.keep + (1 - place) * trade_b.give, half
                    )
                    part[slot, pl.ds(first, half)] = lower(slot, first, half).astype(BF16)

                    @pl.when(place == 0)
                    def _():
                        trade_b.pair(stage).start()

                    return carry

                lax.fori_loop(0, 2, one, 0)
                trade_b.send_sum(stage)

                @pl.when(stage == 0)
                def _():
                    trade_b.pass_on(1)

                return carry

            lax.fori_loop(0, 2, far_slot, 0)
            for number in (4, 5, 6):
                keep(number, at).start()
            trade_b.finish()

            def after(span):
                total = own[span] + got[0, span].astype(F32) + got[2, span].astype(F32)
                branch = total + refs.row_bias[at, 1:2]
                refs.branch_b[at, span] = branch
                stream[span] = stream[span] + refs.layer_scale[at, 1:2] * branch

            each_chunk(rows, after)
            trade_b.drain_gather()
            trade_b.drain_sum()

        @pl.when(at == last)
        def _():
            pltpu.make_async_copy(
                refs.gath_b.at[at, 0], refs.gath_b_kept.at[at, 0], refs.out_sems.at[4, at]
            ).start()
            trade.drain_gather()
            trade.drain_sum()

        return carry

    lax.fori_loop(0, layers, layer, 0)
    for stage in range(2):
        early.arrived(stage)
    early.drain_gather()
    leave = pltpu.make_async_copy(refs.gath_z, refs.gath_z_out, refs.load_sems.at[0])
    leave.start()
    pltpu.make_async_copy(
        refs.gath_b.at[last, 0], refs.gath_b_kept.at[last, 0], refs.out_sems.at[4, last]
    ).wait()
    for at in range(layers):
        for number in range(len(ForwardKept._fields)):
            if at < last or number < 4:
                keep(number, at).wait()
    leave.wait()


def run_forward(lengths, index_rows, rel_table, rows_in, weights, norms):
    tokens, cotangent = rows_in
    rows, width = tokens.shape
    w_qkv, qv_bias, w_out, w_up, fc1_bias, w_down = weights
    layers, _, head_count = rel_table.shape
    wide = w_qkv.shape[2] // 3
    inner = w_up.shape[2]
    in_vmem = pl.BlockSpec(memory_space=pltpu.VMEM)
    in_hbm = pl.BlockSpec(memory_space=pl.ANY)

    def low(*shape):
        return jax.ShapeDtypeStruct(shape, BF16)

    def full(*shape):
        return jax.ShapeDtypeStruct(shape, F32)

    kept = [
        low(layers, 4, *tail)
        for tail in (
            (rows, width),
            (rows, 3 * wide),
            (head_count, rows, rows),
            (rows, wide),
            (rows, width),
            (rows, inner),
            (rows, inner),
        )
    ]
    own = full(rows, width)
    by_layer = full(layers, rows, width)
    near = [low(4, SPAN, rows), low(4, rows, SPAN), own, by_layer, by_layer]
    near += [full(layers, 2, rows, 128), by_layer, by_layer, own]
    scratch = [
        *kept,
        low(4, rows, width),
        low(layers, 4, head_count, rows, rows),
        full(4, rows, rows),
        jax.ShapeDtypeStruct(index_rows.shape, index_rows.dtype),
        low(*w_qkv.shape),
        low(layers, wide, width),
        low(*w_up.shape),
        low(*w_down.shape),
        full(layers, 1, 3 * wide),
        full(layers, 1, inner),
        full(rows, inner),
        low(4, rows, width),
        low(3, rows, width),
        low(rows, width),
        own,
    ]
    copies = 3 * Exchange.COPIES
    return pl.pallas_call(
        functools.partial(forward_body, layers, head_count),
        name="forward",
        out_shape=[*kept, low(4, rows, width), *near],
        in_specs=[pl.BlockSpec(memory_space=pltpu.SMEM)] + [in_vmem] * 9 + [in_hbm] * 5,
        out_specs=[in_hbm] * (len(kept) + 1) + [in_vmem] * len(near),
        scratch_shapes=[
            *[pltpu.VMEM(leaf.shape, leaf.dtype) for leaf in scratch],
            pltpu.SemaphoreType.DMA((copies,)),
            pltpu.SemaphoreType.DMA((copies,)),
            pltpu.SemaphoreType.DMA((4 + layers,)),
            pltpu.SemaphoreType.DMA((len(kept), layers)),
        ],
        compiler_params=pltpu.CompilerParams(
            collective_id=0, has_side_effects=True, vmem_limit_bytes=65400 * 1024
        ),
    )(
        lengths,
        tokens,
        cotangent,
        qv_bias,
        fc1_bias,
        shifted_table(rel_table),
        *norms,
        index_rows,
        w_qkv,
        w_out,
        w_up,
        w_down,
    )


def fold(values):
    return jnp.sum(values.reshape(-1, 8, values.shape[-1]), 0)


def enter_back(grad, branch, scale, gath, sums):
    rows, width = grad.shape

    def body(span, carry):
        values = grad[span]
        gath[0, span] = (values * scale).astype(BF16)
        return carry[0] + fold(values * branch[span]), carry[1] + fold(values)

    step, count = by_chunk(rows, body)
    zero = jnp.zeros((8, width), F32)
    by_branch, alone = lax.fori_loop(0, count, step, (zero, zero))
    sums[2:3] = jnp.sum(by_branch, 0, keepdims=True)
    sums[3:4] = jnp.sum(alone, 0, keepdims=True) * scale


def leave_back(grad, own, got, normal, inverse, gain, sums):
    rows, width = grad.shape

    def body(span, carry):
        total = own[span] + got[0, span].astype(F32) + got[2, span].astype(F32)
        unit = normal[span]
        scaled = total * gain
        centered = (
            scaled
            - jnp.mean(scaled, -1, keepdims=True)
            - unit * jnp.mean(scaled * unit, -1, keepdims=True)
        )
        grad[span] = grad[span] + inverse[span, 0:1] * centered
        return carry[0] + fold(total * unit), carry[1] + fold(total)

    step, count = by_chunk(rows, body)
    zero = jnp.zeros((8, width), F32)
    by_unit, alone = lax.fori_loop(0, count, step, (zero, zero))
    sums[0:1] = jnp.sum(by_unit, 0, keepdims=True)
    sums[1:2] = jnp.sum(alone, 0, keepdims=True)


def weight_grad(left, right, out, start, count, tick=None):
    block = 256
    used = count * block // left.shape[2]

    def step(place, carry):
        span = pl.ds(pl.multiple_of(place * block, block), block)
        total = None
        for slot in range(4):
            term = dot(left[slot, :, span], right[slot], 0, 0)
            total = term if total is None else total + term
        there = pl.ds(pl.multiple_of(start + place * used, 16), used)
        out[there] = total[:used].astype(out.dtype)
        return carry

    if tick is None:
        lax.fori_loop(0, left.shape[2] // block, step, 0)
    else:
        for place in range(left.shape[2] // block):
            step(place, 0)
            tick()


PIECES = 2


class Ticker:
    def __init__(self, ring):
        self.ring = ring
        self.under_way = []

    def add(self, streams):
        self.ring.start(streams)
        self.under_way.append([streams, 0])

    def tick(self):
        if self.under_way:
            self.one()

    def one(self):
        ring = self.ring
        streams, step = self.under_way.pop(0)
        turn = ring.count - 1
        for stream in streams:
            if step < turn:
                ring.add(stream, step)
                ring.copy(stream, step, False).wait_send()
            else:
                ring.copy(stream, step, True).wait_recv()
            if step + 1 < ring.steps:
                ring.copy(stream, step + 1, step + 1 >= turn).start()
        if step + 1 < ring.steps:
            self.under_way.append([streams, step + 1])
        else:
            ring.drain(streams)

    def alike(self, step):
        turn = self.ring.count - 1
        return turn - 1 - step if step < turn else self.ring.steps - 1 - step

    def finish(self):
        ring = self.ring
        turn = ring.count - 1
        while self.under_way:
            run = min(self.alike(step) for _, step in self.under_way)
            if run < 2:
                for _ in range(len(self.under_way)):
                    self.one()
                continue
            rings = list(self.under_way)

            def body(number, carry):
                for streams, start in rings:
                    step = start + number
                    for stream in streams:
                        if start < turn:
                            ring.add(stream, step)
                            ring.copy(stream, step, False).wait_send()
                        else:
                            ring.copy(stream, step, True).wait_recv()
                        ring.copy(stream, step + 1, start >= turn).start()
                return carry

            lax.fori_loop(0, run, body, 0)
            for leaf in self.under_way:
                leaf[1] += run


def mlp_loads(refs, at):
    return load_all(
        (
            (refs.branch_b_all.at[at], refs.branch_b),
            (refs.w_down_all.at[at], refs.w_down),
            (refs.slope_all.at[at], refs.slope),
            (refs.w_up_all.at[at], refs.w_up),
            (refs.normal_b_all.at[at], refs.normal_b),
            (refs.inverse_all.at[at, 1], refs.inverse_b),
            (refs.active_all.at[at], refs.active),
            (refs.gath_b_all.at[at], refs.gath_b),
        ),
        refs.load_sems.at[1 + 2 * at],
    )


def attend_loads(refs, at):
    return load_all(
        (
            (refs.branch_a_all.at[at], refs.branch_a),
            (refs.w_out_all.at[at], refs.w_out.at[pl.ds(0, refs.w_out_all.shape[1])]),
            (refs.qkv_all.at[at], refs.qkv),
            (refs.weights_all.at[at], refs.weights),
            (refs.w_qkv_all.at[at], refs.w_qkv),
            (refs.normal_a_all.at[at], refs.normal_a),
            (refs.inverse_all.at[at, 0], refs.inverse_a),
            (refs.mixture_all.at[at], refs.mixture),
            (refs.gath_a_all.at[at], refs.gath_a),
        ),
        refs.load_sems.at[2 + 2 * at],
    )


def front(refs, group, at, tick, begin):
    rows = refs.grad.shape[0]
    half = rows // 2
    ahead = Exchange(
        group, Exchange.COPIES, refs.gath_b, refs.part_f, refs.got_f, refs.summed_f
    )
    trade = Exchange(group, 0, None, refs.part, refs.got, refs.summed)
    loads = load_all(
        (
            (refs.gath_b_all.at[at, 0], refs.gath_b.at[0]),
            (refs.w_up_all.at[at], refs.w_up),
            (refs.w_down_all.at[at], refs.w_down),
            (refs.gath_z, refs.gath_m),
            (refs.normal_b_all.at[at], refs.normal_b),
            (refs.inverse_all.at[at, 1], refs.inverse_b),
        ),
        refs.load_sems.at[0],
    )
    loads[0].wait()
    ahead.start()
    ahead.spread()
    for load in loads[1:4]:
        load.wait()

    def work(slot):
        refs.hidden[...] = dot(refs.gath_b[slot], refs.w_up[...]) + refs.up_bias[at : at + 1].astype(F32)
        refs.hidden_f[...] = dot(refs.gath_m[slot], refs.w_down[...], 1, 1)

        def act(place, carry):
            span = pl.ds(pl.multiple_of(place * 16, 16), 16)
            high, incline = gelu_parts(refs.hidden[span])
            refs.active[slot, span] = high.astype(BF16)
            back = (refs.hidden_f[span] * incline).astype(BF16)
            refs.d_hidden[slot, span] = back
            refs.up_total[...] += fold(back.astype(F32))
            return carry

        lax.fori_loop(0, rows // 16, act, 0)

    refs.up_total[...] = jnp.zeros_like(refs.up_total)

    def chip_slot(slot, carry):
        work(slot)
        result = dot(refs.d_hidden[slot], refs.w_up[...], 1, 1)
        result_f = dot(refs.active[slot], refs.w_down[...])

        @pl.when(slot == 0)
        def _():
            refs.own[...] = result
            refs.own_f[...] = result_f

        @pl.when(slot == 1)
        def _():
            refs.part[1] = result.astype(BF16)
            refs.part_f[1] = result_f.astype(BF16)

        return carry

    lax.fori_loop(0, 2, chip_slot, 0)
    trade.sum_near().start()
    ahead.sum_near().start()
    ahead.pass_on(0)

    def far_slot(stage, carry):
        slot = ahead.slot(stage)
        ahead.arrived(stage)
        work(slot)

        def one(place, carry):
            first = pl.multiple_of(place * ahead.keep + (1 - place) * ahead.give, half)
            span = pl.ds(first, half)
            refs.part[slot, span] = dot(
                refs.d_hidden[slot, span], refs.w_up[...], 1, 1
            ).astype(BF16)

            @pl.when(place == 0)
            def _():
                trade.pair(stage).start()

            refs.part_f[slot, span] = dot(refs.active[slot, span], refs.w_down[...]).astype(BF16)

            @pl.when(place == 0)
            def _():
                ahead.pair(stage).start()

            return carry

        lax.fori_loop(0, 2, one, 0)
        trade.send_sum(stage)
        ahead.send_sum(stage)

        @pl.when(stage == 0)
        def _():
            ahead.pass_on(1)

        return carry

    lax.fori_loop(0, 2, far_slot, 0)
    data, inner = refs.data_m.at[at], refs.w_down.shape[0]
    weight_grad(refs.active, refs.gath_m, data, 0, inner)
    weight_grad(refs.gath_b, refs.d_hidden, data, inner, refs.w_up.shape[0])
    begin(at, 0)
    refs.up_sums[at : at + 1] = jnp.sum(refs.up_total[...], 0, keepdims=True)
    for load in loads[4:]:
        load.wait()
    trade.finish()
    tick()
    leave_back(
        refs.grad,
        refs.own,
        refs.got,
        refs.normal_b,
        refs.inverse_b,
        refs.ln_gain[at, 1:2],
        refs.sums.at[2 * at + 1],
    )
    ahead.drain_gather()
    trade.drain_sum()

    def end():
        ahead.finish()
        sums = refs.sums.at[2 * at + 1]
        scale = refs.layer_scale[at, 1:2]
        width = refs.grad.shape[1]

        def body(span, carry):
            branch = (
                refs.own_f[span]
                + refs.got_f[0, span].astype(F32)
                + refs.got_f[2, span].astype(F32)
                + refs.row_bias[at, 1:2]
            )
            refs.stream[span] = refs.middle[span] + scale * branch
            values = refs.grad_in[span]
            return carry[0] + fold(values * branch), carry[1] + fold(values)

        step, count = by_chunk(rows, body)
        zero = jnp.zeros((8, width), F32)
        by_branch, alone = lax.fori_loop(0, count, step, (zero, zero))
        sums[2:3] = jnp.sum(by_branch, 0, keepdims=True)
        sums[3:4] = jnp.sum(alone, 0, keepdims=True) * scale
        ahead.drain_sum()

    return end


def back_mlp(refs, group, base, at, loads, tick, begin):
    rows = refs.grad.shape[0]
    half = rows // 2
    gath, part, hidden, d_hidden = refs.gath_m, refs.part, refs.hidden, refs.d_hidden
    trade = Exchange(group, base, gath, part, refs.got, refs.summed)
    sums = refs.sums.at[2 * at + 1]
    loads[0].wait()
    enter_back(refs.grad, refs.branch_b, refs.layer_scale[at, 1:2], gath, sums)
    trade.start()
    tick()
    trade.spread()
    for load in loads[1:4]:
        load.wait()

    refs.up_total[...] = jnp.zeros_like(refs.up_total)

    def down(slot):
        hidden[...] = dot(gath[slot], refs.w_down[...], 1, 1)

        def body(place, carry):
            span = pl.ds(pl.multiple_of(place * CHUNK, CHUNK), CHUNK)
            low = (hidden[span] * refs.slope[slot, span].astype(F32)).astype(BF16)
            d_hidden[slot, span] = low
            return carry + fold(low.astype(F32))

        zero = jnp.zeros((8, hidden.shape[1]), F32)
        refs.up_total[...] += lax.fori_loop(0, rows // CHUNK, body, zero)

    def back(slot, first, count):
        return dot(d_hidden[slot, pl.ds(first, count)], refs.w_up[...], 1, 1)

    down(0)
    tick()
    refs.own[...] = back(0, 0, rows)
    tick()
    down(1)
    part[1] = back(1, 0, rows).astype(BF16)
    trade.sum_near().start()
    tick()
    trade.pass_on(0)
    for stage in range(2):
        slot = trade.slot(stage)
        trade.arrived(stage)
        down(slot)
        tick()

        def one(place, carry):
            first = pl.multiple_of(place * trade.keep + (1 - place) * trade.give, half)
            part[slot, pl.ds(first, half)] = back(slot, first, half).astype(BF16)

            @pl.when(place == 0)
            def _():
                trade.pair(stage).start()

            return carry

        lax.fori_loop(0, 2, one, 0)
        trade.send_sum(stage)
        if stage == 0:
            trade.pass_on(1)
        tick()
    refs.up_sums[at : at + 1] = jnp.sum(refs.up_total[...], 0, keepdims=True)
    for load in loads[4:]:
        load.wait()
    data, inner = refs.data_m.at[at], refs.w_down.shape[0]
    weight_grad(refs.active, gath, data, 0, inner)
    tick()
    weight_grad(refs.gath_b, d_hidden, data, inner, refs.w_up.shape[0])
    begin(at, 0)
    tick()
    trade.finish()
    leave_back(
        refs.grad,
        refs.own,
        refs.got,
        refs.normal_b,
        refs.inverse_b,
        refs.ln_gain[at, 1:2],
        sums,
    )
    trade.drain_gather()
    trade.drain_sum()
    tick()


def back_attend(refs, group, base, at, head_count, loads, tick, begin, meanwhile):
    rows = refs.grad.shape[0]
    half = rows // 2
    data = refs.data_t.at[at]
    wide = refs.mixture.shape[2]
    gath, part, d_mixed, d_scores = refs.gath_t, refs.part, refs.d_mixed, refs.d_scores
    qkv = refs.qkv
    trade = Exchange(group, base, gath, part, refs.got, refs.summed)
    sums = refs.sums.at[2 * at]
    loads[0].wait()
    enter_back(refs.grad, refs.branch_a, refs.layer_scale[at, 0:1], gath, sums)
    trade.start()
    tick()
    trade.spread()
    if meanwhile is not None:
        meanwhile()
        tick()
    for load in loads[1:5]:
        load.wait()
    spare = jnp.zeros((rows, wide - head_count * HEAD_DIM), BF16)

    def attend(slot):
        d_mix = dot(gath[slot], refs.w_out[...], 1, 1).astype(BF16)
        pieces = ([], [], [])
        for head in range(head_count):
            lanes = slice(head * HEAD_DIM, (head + 1) * HEAD_DIM)
            queries = qkv[slot, :, 0:wide][:, lanes]
            keys = qkv[slot, :, wide : 2 * wide][:, lanes]
            values = qkv[slot, :, 2 * wide : 3 * wide][:, lanes]
            share = refs.weights[slot, head]
            d_head = d_mix[:, lanes]
            wide_share = share.astype(F32)
            d_share = dot(d_head, values, 1, 1)
            middle = jnp.sum(wide_share * d_share, -1, keepdims=True)
            d_score = (wide_share * (d_share - middle)).astype(BF16)
            d_scores[slot, head] = d_score
            pieces[0].append((dot(d_score, keys) * HEAD_DIM**-0.5).astype(BF16))
            pieces[1].append(dot(d_score, queries, 0, 0).astype(BF16))
            pieces[2].append(dot(share, d_head, 0, 0).astype(BF16))
        for place in range(3):
            d_mixed[slot, :, place * wide : (place + 1) * wide] = jnp.concatenate(
                pieces[place] + [spare], -1
            )

    def back(slot, first, count):
        return dot(d_mixed[slot, pl.ds(first, count)], refs.w_qkv[...], 1, 1)

    attend(0)
    tick()
    refs.own[...] = back(0, 0, rows)
    attend(1)
    tick()
    part[1] = back(1, 0, rows).astype(BF16)
    trade.sum_near().start()
    trade.pass_on(0)
    for stage in range(2):
        slot = trade.slot(stage)
        trade.arrived(stage)
        attend(slot)
        tick()

        def one(place, carry):
            first = pl.multiple_of(place * trade.keep + (1 - place) * trade.give, half)
            part[slot, pl.ds(first, half)] = back(slot, first, half).astype(BF16)

            @pl.when(place == 0)
            def _():
                trade.pair(stage).start()

            return carry

        lax.fori_loop(0, 2, one, 0)
        trade.send_sum(stage)
        if stage == 0:
            trade.pass_on(1)
        tick()
    for load in loads[5:]:
        load.wait()

    def add(slot, total):
        def body(span, carry):
            return carry + fold(d_mixed[slot, span].astype(F32))

        step, count = by_chunk(rows, body)
        return lax.fori_loop(0, count, step, total)

    total = jnp.zeros((8, 3 * wide), F32)
    for slot in range(4):
        total = add(slot, total)
    refs.qkv_sums[at : at + 1] = jnp.sum(total, 0, keepdims=True)
    used = 3 * head_count * HEAD_DIM
    weight_grad(d_mixed, refs.gath_a, data, 0, used)
    tick()
    weight_grad(refs.mixture, gath, data, used, used // 3)
    begin(at, 1)
    tick()
    for head in range(head_count):
        total = None
        for slot in range(4):
            placed = dot(refs.spots[slot], d_scores[slot, head]).astype(BF16)
            term = dot(placed, refs.turned[slot])
            total = term if total is None else total + term
        row = at * head_count + head
        refs.table_sums[row : row + 1] = table_row(total)
    trade.finish()
    leave_back(
        refs.grad,
        refs.own,
        refs.got,
        refs.normal_a,
        refs.inverse_a,
        refs.ln_gain[at, 0:1],
        sums,
    )
    trade.drain_gather()
    trade.drain_sum()
    tick()


class BackInputs(NamedTuple):
    grad_in: object
    middle: object
    branch_a_all: object
    branch_b_all: object
    normal_a_all: object
    normal_b_all: object
    inverse_all: object
    mixture_all: object
    qkv_all: object
    weights_all: object
    gath_a_all: object
    active_all: object
    slope_all: object
    gath_b_all: object
    gath_z: object
    w_qkv_all: object
    w_out_all: object
    w_up_all: object
    w_down_all: object
    spots: object
    turned: object
    up_bias: object
    ln_gain: object
    layer_scale: object
    row_bias: object


class BackOutputs(NamedTuple):
    grad: object
    stream: object
    d_qkv: object
    d_out: object
    d_up: object
    d_down: object
    small_out: object


class BackScratch(NamedTuple):
    branch_a: object
    branch_b: object
    normal_a: object
    normal_b: object
    own: object
    own_f: object
    inverse_a: object
    inverse_b: object
    mixture: object
    qkv: object
    weights: object
    gath_a: object
    active: object
    slope: object
    gath_b: object
    gath_m: object
    gath_t: object
    w_qkv: object
    w_out: object
    w_up: object
    w_down: object
    d_hidden: object
    hidden: object
    hidden_f: object
    d_mixed: object
    d_scores: object
    part: object
    part_f: object
    got: object
    got_f: object
    summed: object
    summed_f: object
    sums: object
    up_total: object
    up_sums: object
    qkv_sums: object
    table_sums: object
    lines: object
    near_got: object
    pair_sum: object
    far_got: object
    data_m: object
    data_t: object
    got_m: object
    got_t: object
    small: object
    got_small: object
    send_sems: object
    recv_sems: object
    load_sems: object
    ring_send_m: object
    ring_recv_m: object
    ring_send_t: object
    ring_recv_t: object
    ring_send_s: object
    ring_recv_s: object
    out_sems: object


def backward_body(layers, head_count, count, *all_refs):
    refs = Names((*BackInputs._fields, *BackOutputs._fields, *BackScratch._fields), all_refs)
    rows, width = refs.grad.shape
    last = layers - 1
    group = Group(refs.send_sems, refs.recv_sems)
    barrier = pltpu.get_barrier_semaphore()
    greeted = group.greet(barrier)
    ring = Ring(count) if count else None
    if ring:
        for other in ring.sides:
            pl.semaphore_signal(barrier, inc=1, device_id={"dp": other}, device_id_type=MESH)
        greeted += 2
    pl.semaphore_wait(barrier, greeted)
    ticker = Ticker(ring)

    def begin(at, kind):
        if not ring:
            return
        leaf = (
            (refs.data_m, refs.got_m, refs.ring_send_m, refs.ring_recv_m),
            (refs.data_t, refs.got_t, refs.ring_send_t, refs.ring_recv_t),
        )[kind]
        streams = ring.streams(tuple(ref.at[at] for ref in leaf))
        for first in range(0, len(streams), 2):
            ticker.add(streams[first : first + 2])

    refs.grad[...] = refs.grad_in[...]
    refs.w_out[refs.w_out_all.shape[1] :] = jnp.zeros_like(refs.w_out[refs.w_out_all.shape[1] :])
    end = front(refs, group, last, ticker.tick, begin)
    loads_m = None
    for at in reversed(range(layers)):
        base = (2 + 2 * at) * Exchange.COPIES
        if at < last:
            back_mlp(refs, group, base, at, loads_m, ticker.tick, begin)
        loads_t = attend_loads(refs, at)
        if at:
            loads_m = mlp_loads(refs, at - 1)
        back_attend(
            refs,
            group,
            base + Exchange.COPIES,
            at,
            head_count,
            loads_t,
            ticker.tick,
            begin,
            end if at == last else None,
        )

    shared = 8 * layers
    lines = refs.lines
    lines[...] = jnp.zeros_like(lines)
    for kind in range(4):
        for at in range(2 * layers):
            row = kind * 2 * layers + at
            lines[row : row + 1] = refs.sums[at, kind : kind + 1]
    base = (2 + 2 * layers) * Exchange.COPIES
    first = group.copy(base, base, lines.at[pl.ds(0, shared)], refs.near_got, group.near)
    first.start()
    ticker.tick()
    first.wait_recv()
    refs.pair_sum[...] = lines[0:shared] + refs.near_got[...]
    second = group.copy(base + 1, base + 1, refs.pair_sum, refs.far_got, group.far)
    second.start()
    ticker.tick()
    second.wait_recv()
    first.wait_send()
    lines[0:shared] = refs.pair_sum[...] + refs.far_got[...]
    row = shared
    for leaf, height in (
        (refs.qkv_sums, layers),
        (refs.up_sums, layers),
        (refs.table_sums, layers * head_count),
    ):
        lines[row : row + height] = leaf[0:height]
        row += height
    cuts = [
        (slice(at * SMALL_ROWS, (at + 1) * SMALL_ROWS), slice(at * 128, (at + 1) * 128))
        for at in range(width // 128)
    ]
    used = refs.d_qkv.shape[1]
    leaves = []

    def leave(at):
        for source, first, target in (
            (refs.data_m, 0, refs.d_down),
            (refs.data_m, refs.d_down.shape[1], refs.d_up),
            (refs.data_t, 0, refs.d_qkv),
            (refs.data_t, used, refs.d_out),
        ):
            step = pltpu.make_async_copy(
                source.at[at, pl.ds(first, target.shape[1])],
                target.at[at],
                refs.out_sems.at[len(leaves)],
            )
            step.start()
            leaves.append(step)

    if ring:
        small = refs.small
        small[...] = jnp.zeros_like(small)
        for rows_at, lanes in cuts:
            small[rows_at] = lines[:, lanes]
        ticker.add(
            ring.streams((small, refs.got_small, refs.ring_send_s, refs.ring_recv_s))
        )
        ticker.finish()
    for at in reversed(range(layers)):
        leave(at)
    second.wait_send()
    if ring:
        for rows_at, lanes in cuts:
            refs.small_out[:, lanes] = small[rows_at]
    else:
        refs.small_out[...] = lines[...]
    for step in leaves:
        step.wait()


def run_backward(count, inputs, head_count):
    grad, w_out, w_up = inputs[0], inputs[16], inputs[17]
    rows, width = grad.shape
    layers, wide = w_out.shape[0], inputs[15].shape[2] // 3
    inner = w_up.shape[2]
    used = head_count * HEAD_DIM
    ring_count = count or 2
    steps = 2 * (ring_count - 1)
    in_vmem = pl.BlockSpec(memory_space=pltpu.VMEM)
    in_hbm = pl.BlockSpec(memory_space=pl.ANY)
    assert inner == width == 3 * wide == 4 * used and layers == 2

    def wide_rows(*shape):
        return pltpu.VMEM(shape, F32)

    def low(*shape):
        return pltpu.VMEM(shape, BF16)

    def sems(*shape):
        return pltpu.SemaphoreType.DMA(shape)

    def ring_got(total, pieces):
        piece = total // (2 * ring_count * pieces)
        return low(layers, 2, pieces, ring_count - 1, piece, width)

    own = wide_rows(rows, width)
    four = low(4, rows, width)
    square = low(4, head_count, rows, rows)
    lines = wide_rows(8 * layers, width)
    small_rows = -(-SMALL_ROWS * (width // 128) // (16 * ring_count)) * 16 * ring_count
    exchanges = (2 + 2 * layers) * Exchange.COPIES + 2
    scratch = (
        [own] * 6
        + [wide_rows(rows, 128)] * 2
        + [low(4, rows, wide), four, square, four, four, four, four, four, four]
        + [low(width, 3 * wide), low(wide, width), low(width, inner), low(inner, width)]
        + [four, own, own, four, square, four, four]
        + [low(3, rows, width)] * 2
        + [low(rows, width)] * 2
        + [wide_rows(2 * layers, 8, width)]
        + [wide_rows(8, width)] * 4
        + [wide_rows(SMALL_ROWS, width), lines, lines, lines]
        + [low(layers, 2 * width, width), low(layers, width, width)]
        + [ring_got(2 * width, PIECES), ring_got(width, 1)]
        + [wide_rows(small_rows, 128)]
        + [wide_rows(2, 1, ring_count - 1, small_rows // (2 * ring_count), 128)]
        + [sems(exchanges)] * 2
        + [sems(1 + 2 * layers, 9)]
        + [sems(layers, 2, PIECES, steps)] * 2
        + [sems(layers, 2, 1, steps)] * 2
        + [sems(2, 1, steps)] * 2
        + [sems(4 * layers)]
    )
    return pl.pallas_call(
        functools.partial(backward_body, layers, head_count, count),
        name="backward",
        out_shape=[
            jax.ShapeDtypeStruct((rows, width), F32),
            jax.ShapeDtypeStruct((rows, width), F32),
            jax.ShapeDtypeStruct((layers, 3 * used, width), BF16),
            jax.ShapeDtypeStruct((layers, used, width), BF16),
            jax.ShapeDtypeStruct((layers, width, inner), BF16),
            jax.ShapeDtypeStruct((layers, inner, width), BF16),
            jax.ShapeDtypeStruct((SMALL_ROWS, width), F32),
        ],
        in_specs=[in_vmem] * 2 + [in_hbm] * 17 + [in_vmem] * 6,
        out_specs=[in_vmem] * 2 + [in_hbm] * 4 + [in_vmem],
        scratch_shapes=scratch,
        compiler_params=pltpu.CompilerParams(
            collective_id=1, has_side_effects=True, vmem_limit_bytes=65400 * 1024
        ),
    )(*inputs)


SMALL_ROWS = 32


class Ring:
    def __init__(self, count):
        self.count = count
        self.steps = 2 * (count - 1)
        self.place = self.place_of(lax.axis_index("dp"))
        self.sides = (
            self.number_of((self.place + 1) % count),
            self.number_of((self.place + count - 1) % count),
        )

    def place_of(self, number):
        row, side = number // 2, number % 2
        return row + side * (self.count - 1 - 2 * row)

    def number_of(self, place):
        side = place // (self.count // 2)
        return 2 * (place + side * (self.count - 1 - 2 * place)) + side

    def streams(self, *sets):
        return [
            (leaf, way, sub)
            for leaf in sets
            for sub in range(leaf[1].shape[1])
            for way in range(2)
        ]

    def rows(self, stream, step):
        (data, got, _, _), way, sub = stream
        subs, piece = got.shape[1], got.shape[3]
        if way == 0:
            chunk = (self.place + 3 * self.count - step) % self.count
        else:
            chunk = (self.place + step) % self.count
        first = ((way * self.count + chunk) * subs + sub) * piece
        return pl.ds(pl.multiple_of(first, piece), piece)

    def copy(self, stream, step, gather):
        (data, got, send_sems, recv_sems), way, sub = stream
        rows = self.rows(stream, step)
        return pltpu.make_async_remote_copy(
            src_ref=data.at[rows],
            dst_ref=data.at[rows] if gather else got.at[way, sub, step],
            send_sem=send_sems.at[way, sub, step],
            recv_sem=recv_sems.at[way, sub, step],
            device_id={"dp": self.sides[way]},
            device_id_type=MESH,
        )

    def start(self, streams):
        for stream in streams:
            self.copy(stream, 0, False).start()

    def add(self, stream, step):
        (data, got, _, _), way, sub = stream
        self.copy(stream, step, False).wait_recv()
        rows = self.rows(stream, step + 1)
        data[rows] = data[rows] + got[way, sub, step]

    def drain(self, streams):
        for step in range(self.count - 1, self.steps):
            for stream in streams:
                self.copy(stream, step, True).wait_send()


def ring_fits(count, rows):
    return count == 8 and rows % (2 * count * 16) == 0


def widen_body(
    wide,
    lengths,
    stream,
    gradient,
    out_in,
    up_in,
    down_in,
    small,
    result,
    d_tokens,
    d_out,
    d_up,
    d_down,
    d_bias,
    d_up_bias,
    *kinds,
):
    number = pl.program_id(0)
    rows, width = stream.shape
    layers, _, used = d_bias.shape
    place = lax.axis_index("tensor")
    length = lengths[place, 0] + lengths[place, 1]
    row = number * rows + lax.broadcasted_iota(jnp.int32, (rows, width), 0)
    result[...] = jnp.where(row < length, stream[...], 0.0).astype(BF16)
    d_tokens[...] = gradient[...]
    d_out[...] = out_in[...].astype(F32)
    d_up[...] = up_in[...].astype(F32)
    d_down[...] = down_in[...].astype(F32)

    @pl.when(number == 0)
    def _():
        for kind, leaf in enumerate(kinds):
            for at in range(layers):
                first = 2 * (kind * layers + at)
                leaf[at] = small[first : first + 2]
        first = 8 * layers
        for at in range(layers):
            for half in range(2):
                start = 2 * half * wide
                d_bias[at, half : half + 1] = small[
                    first + at : first + at + 1, start : start + used
                ]
        first += layers
        d_up_bias[...] = small[first : first + layers]


def run_widen(lengths, stream, gradient, d_out, d_up, d_down, small, wide, used):
    rows, width = stream.shape
    layers = d_out.shape[0]
    parts = 4
    steps = layers * parts

    def rows_of(total):
        return pl.BlockSpec((total // steps, width), lambda at: (at, 0))

    def block(leaf):
        return pl.BlockSpec(
            (1, leaf.shape[1] // parts, width), lambda at: (at // parts, at % parts, 0)
        )

    def whole(*shape):
        return pl.BlockSpec(shape, lambda at: (0,) * len(shape))

    def full(*shape):
        return jax.ShapeDtypeStruct(shape, F32)

    return pl.pallas_call(
        functools.partial(widen_body, wide),
        name="widen",
        grid=(steps,),
        out_shape=[
            jax.ShapeDtypeStruct((rows, width), BF16),
            full(rows, width),
            full(*d_out.shape),
            full(*d_up.shape),
            full(*d_down.shape),
            full(layers, 2, used),
            full(layers, width),
            *[full(layers, 2, width)] * 4,
        ],
        in_specs=[
            pl.BlockSpec(memory_space=pltpu.SMEM),
            rows_of(rows),
            rows_of(rows),
            block(d_out),
            block(d_up),
            block(d_down),
            whole(*small.shape),
        ],
        out_specs=[
            rows_of(rows),
            rows_of(rows),
            block(d_out),
            block(d_up),
            block(d_down),
            whole(layers, 2, used),
            whole(layers, width),
            *[whole(layers, 2, width)] * 4,
        ],
    )(lengths, stream, gradient, d_out, d_up, d_down, small)


def per_device(
    tokens,
    cotangent,
    segments,
    lengths,
    rel_index,
    w_qkv,
    qv_bias,
    w_out,
    w_fc1,
    fc1_bias,
    w_fc2,
    rel_table,
    ln_gain,
    ln_bias,
    layer_scale,
    row_bias,
):
    own_rows, width = tokens.shape
    group_rows, bin_rows = rel_index.shape
    layer_count = w_qkv.shape[0]
    head_count = rel_table.shape[2]
    local_width = w_qkv.shape[3]
    wide = -(-local_width // 256) * 256
    bin_total = group_rows // bin_rows
    place = lax.axis_index("tensor")
    assert own_rows == bin_rows and bin_total == 4

    extra = wide - local_width
    qkv_used = jnp.pad(w_qkv, ((0, 0), (0, 0), (0, 0), (0, extra))).reshape(
        layer_count, width, 3 * wide
    )
    norms = (ln_gain, ln_bias, layer_scale, row_bias)

    (
        gath_a,
        qkv,
        shares,
        mixture,
        gath_b,
        slope,
        active,
        gath_z,
        spots,
        turned,
        gradient,
        normal_a,
        normal_b,
        inverse,
        branch_a,
        branch_b,
        middle,
    ) = run_forward(
        lengths,
        rel_index,
        rel_table,
        (tokens, cotangent),
        (qkv_used, qv_bias, w_out, w_fc1, fc1_bias, w_fc2),
        norms,
    )
    dp_count = lax.axis_size("dp")
    with_ring = ring_fits(dp_count, width)
    gradient, stream, *sums = run_backward(
        dp_count if with_ring else None,
        (
            gradient,
            middle,
            branch_a,
            branch_b,
            normal_a,
            normal_b,
            inverse,
            mixture,
            qkv,
            shares,
            gath_a,
            active,
            slope,
            gath_b,
            gath_z,
            qkv_used,
            w_out,
            w_fc1,
            w_fc2,
            spots,
            turned,
            fc1_bias,
            ln_gain,
            layer_scale,
            row_bias,
        ),
        head_count,
    )
    if not with_ring:
        sums = lax.psum(sums, "dp")
    *weight_sums, small = sums
    d_qkv, d_out, d_up, d_down = weight_sums
    result, d_tokens, d_out, d_up, d_down, d_bias, d_up_bias, *kinds = run_widen(
        lengths, stream, gradient, d_out, d_up, d_down, small, wide, local_width
    )
    d_qkv = jnp.transpose(
        d_qkv.astype(F32).reshape(layer_count, 3, local_width, width), (0, 3, 1, 2)
    )
    first = 8 * layer_count + 2 * layer_count
    d_table = small[first : first + layer_count * head_count, : rel_table.shape[1]]
    d_table = jnp.transpose(d_table.reshape(layer_count, head_count, -1), (0, 2, 1))
    return (
        result,
        d_tokens,
        d_qkv,
        d_bias,
        d_out,
        d_up,
        d_up_bias,
        d_down,
        d_table,
        *kinds,
    )


def solution(mesh):
    in_specs = (
        P(("dp", "tensor"), None),
        P(("dp", "tensor"), None),
        P("dp"),
        P("dp", None),
        P("dp", None),
        P(None, None, None, "tensor"),
        P(None, None, "tensor"),
        P(None, "tensor", None),
        P(None, None, "tensor"),
        P(None, "tensor"),
        P(None, "tensor", None),
        P(None, None, "tensor"),
        P(),
        P(),
        P(),
        P(),
    )
    out_specs = (
        P(("dp", "tensor"), None),
        P(("dp", "tensor"), None),
        P(None, None, None, "tensor"),
        P(None, None, "tensor"),
        P(None, "tensor", None),
        P(None, None, "tensor"),
        P(None, "tensor"),
        P(None, "tensor", None),
        P(None, None, "tensor"),
        P(),
        P(),
        P(),
        P(),
    )
    return jax.shard_map(
        per_device, mesh=mesh, in_specs=in_specs, out_specs=out_specs, check_vma=False
    )
```

profile of v0, /device:TPU:0, one launch (start us, length us, event | category | flops | bytes accessed | tf_op | source)
XLA Modules:
  0.0 303.3 jit_solution(11242086980624429138)
XLA Ops:
  0.6 1.3 copy.37.all_refs_0_.lengths
  1.9 0.7 copy.33
  2.7 0.7 pad_convert_fusion.all_refs_5_
  3.4 1.6 pad.12
  5.0 2.4 copy.35.all_refs_11_.all_refs_15_
  7.4 84.5 %forward.1 = (bf16[2,4,256,768]{3,2,1,0:T(8,128)(2,1)}, bf16[2,4,256,768]{3,2,1,0:T(8,128)(2,1)}, bf16[2,4,3,256,256]{4,3,2,1,0:T(8,128)(2,1)}, bf16[2,4,256,256...) custom-call(s32[4,2]{1,0:T(4,128)} %copy.37.all_refs_0_.lengths, ...), custom_call_target="tpu_custom_call" | custom-call | tf_op jit(solution)/shard_map/forward/pallas_call | solution.py:737
  91.9 196.9 %backward.1 = (f32[256,768]{1,0:T(8,128)}, f32[256,768]{1,0:T(8,128)}, bf16[2,576,768]{2,1,0:T(8,128)(2,1)}, bf16[2,192,768]{2,1,0:T(8,128)(2,1)}, bf16[2,768,76...) custom-call(f32[256,768]{1,0:T(8,128)} %get-tuple-element.48.all_refs_0_, ...), custom_call_target="tpu_custom_call" | custom-call | tf_op jit(solution)/shard_map/backward/pallas_call | solution.py:1550
  288.8 0.8 slice.3
  289.6 0.6 copy.38
  290.3 3.6 %convert_bitcast_fusion = f32[2,768,3,192]{1,3,2,0:T(8,128)} fusion(bf16[2,3,192,768]{3,2,1,0:T(8,128)(2,1)} %bitcast.8), kind=kLoop, calls=%fused_computation | loop fusion | flops 884736 | bytes 5308416 | tf_op jit(solution)/shard_map/transpose | solution.py:1845
  293.8 9.3 %widen.1 = (bf16[256,768]{1,0:T(8,128)(2,1)}, f32[256,768]{1,0:T(8,128)}, f32[2,192,768]{2,1,0:T(8,128)}, f32[2,768,768]{2,1,0:T(8,128)}, f32[2,768,768]{2,1,0:T...) custom-call(s32[4,2]{1,0:T(4,128)} %copy.37.all_refs_0_.lengths, ...), custom_call_target="tpu_custom_call" | custom-call | tf_op jit(solution)/shard_map/widen/pallas_call | solution.py:1709
  (2 shorter events, 0.0 us)
where the time goes:
time: 304 us; the launch traced here: 303 us
  Pallas kernels  291 us (96%)
  local copies, waits for them, and re-layouts  7.53 us (2%)
  other arithmetic  4.27 us (1%)
    pallas_call x1, Pallas kernels, run_backward(): pl.pallas_call(functools.partial(backward_body, layers, head_count, count...  197 us
    pallas_call x1, Pallas kernels, run_forward(): pl.pallas_call(functools.partial(forward_body, layers, head_count), name=...  84.5 us
    pallas_call x1, Pallas kernels, run_widen(): pl.pallas_call(functools.partial(widen_body, wide), name='widen', grid=(s...  9.29 us

commit v1 on v0

--- a/solution.py
+++ b/solution.py
@@ -499,57 +499,66 @@
             attend_rows(refs, at, slot, first, head_count)
             return dot(refs.mixture[at, slot, pl.ds(first, half)], refs.w_out[at])
 
-        def chip_slot(slot, carry):
-            project(slot)
-
-            def one(place, carry):
-                first = pl.multiple_of(place * half, half)
-                result = attend(slot, first)
-
-                @pl.when(slot == 0)
-                def _():
-                    own[pl.ds(first, half)] = result
-
-                @pl.when(slot == 1)
-                def _():
-                    part[1, pl.ds(first, half)] = result.astype(BF16)
-
-                return carry
-
-            lax.fori_loop(0, 2, one, 0)
-            return carry
-
-        lax.fori_loop(0, 2, chip_slot, 0)
-        trade.sum_near().start()
-        trade.pass_on(0)
-
-        def far_slot(stage, carry):
-            slot = trade.slot(stage)
-            trade.arrived(stage)
+        turn = 2 * (at == 0).astype(jnp.int32)
+
+        @pl.when(at == 0)
+        def _():
+            trade.pass_on(0)
+            trade.pass_on(1)
+
+        def one_slot(number, carry):
+            role = (number + turn) % 4
+            stage = role % 2
+            away = role >= 2
+            slot = jnp.where(away, trade.slot(stage), role)
+
+            @pl.when(away)
+            def _():
+                trade.arrived(stage)
+
             project(slot)
 
             def one(place, carry):
                 first = pl.multiple_of(
                     place * trade.keep + (1 - place) * trade.give, half
                 )
-                part[slot, pl.ds(first, half)] = attend(slot, first).astype(BF16)
-
-                @pl.when(place == 0)
+                result = attend(slot, first)
+
+                @pl.when(role == 0)
+                def _():
+                    own[pl.ds(first, half)] = result
+
+                @pl.when(role > 0)
+                def _():
+                    part[slot, pl.ds(first, half)] = result.astype(BF16)
+
+                @pl.when(away & (place == 0))
                 def _():
                     trade.pair(stage).start()
 
                 return carry
 
             lax.fori_loop(0, 2, one, 0)
-            trade.send_sum(stage)
-
-            @pl.when(stage == 0)
+
+            @pl.when(away)
+            def _():
+                trade.send_sum(stage)
+
+            @pl.when(role == 1)
+            def _():
+                trade.sum_near().start()
+
+            @pl.when((at > 0) & (role == 1))
+            def _():
+                trade.pass_on(0)
+
+            @pl.when((at > 0) & (role == 2))
             def _():
                 trade.pass_on(1)
 
             return carry
 
-        lax.fori_loop(0, 2, far_slot, 0)
+        lax.fori_loop(0, 4, one_slot, 0)
         for number in range(4):
             keep(number, at).start()
 
@@ -598,51 +607,55 @@
             def lower(slot, first, count):
                 return dot(refs.active[at, slot, pl.ds(first, count)], refs.w_down[at])
 
-            def chip_slot(slot, carry):
-                raise_rows(slot)
-                result = lower(slot, 0, rows)
-
-                @pl.when(slot == 0)
+            def one_slot(role, carry):
+                stage = role % 2
+                away = role >= 2
+                slot = jnp.where(away, trade_b.slot(stage), role)
+
+                @pl.when(away)
                 def _():
-                    own[...] = result
-
-                @pl.when(slot == 1)
-                def _():
-                    part[1] = result.astype(BF16)
-
-                return carry
-
-            lax.fori_loop(0, 2, chip_slot, 0)
-            trade_b.sum_near().start()
-            trade_b.pass_on(0)
-
-            def far_slot(stage, carry):
-                slot = trade_b.slot(stage)
-                trade_b.arrived(stage)
+                    trade_b.arrived(stage)
+
                 raise_rows(slot)
 
                 def one(place, carry):
                     first = pl.multiple_of(
                         place * trade_b.keep + (1 - place) * trade_b.give, half
                     )
-                    part[slot, pl.ds(first, half)] = lower(slot, first, half).astype(BF16)
-
-                    @pl.when(place == 0)
+                    result = lower(slot, first, half)
+
+                    @pl.when(role == 0)
+                    def _():
+                        own[pl.ds(first, half)] = result
+
+                    @pl.when(role > 0)
+                    def _():
+                        part[slot, pl.ds(first, half)] = result.astype(BF16)
+
+                    @pl.when(away & (place == 0))
                     def _():
                         trade_b.pair(stage).start()
 
                     return carry
 
                 lax.fori_loop(0, 2, one, 0)
-                trade_b.send_sum(stage)
-
-                @pl.when(stage == 0)
+
+                @pl.when(away)
+                def _():
+                    trade_b.send_sum(stage)
+
+                @pl.when(role == 1)
+                def _():
+                    trade_b.sum_near().start()
+                    trade_b.pass_on(0)
+
+                @pl.when(role == 2)
                 def _():
                     trade_b.pass_on(1)
 
                 return carry
 
-            lax.fori_loop(0, 2, far_slot, 0)
+            lax.fori_loop(0, 4, one_slot, 0)
             for number in (4, 5, 6):
                 keep(number, at).start()
             trade_b.finish()
@@ -1027,8 +1040,9 @@
     lax.fori_loop(0, 2, far_slot, 0)
     data, inner = refs.data_m.at[at], refs.w_down.shape[0]
     weight_grad(refs.active, refs.gath_m, data, 0, inner)
+    begin(at, 0, 0)
     weight_grad(refs.gath_b, refs.d_hidden, data, inner, refs.w_up.shape[0])
-    begin(at, 0)
+    begin(at, 0, 1)
     refs.up_sums[at : at + 1] = jnp.sum(refs.up_total[...], 0, keepdims=True)
     for load in loads[4:]:
         load.wait()
@@ -1139,9 +1153,10 @@
         load.wait()
     data, inner = refs.data_m.at[at], refs.w_down.shape[0]
     weight_grad(refs.active, gath, data, 0, inner)
+    begin(at, 0, 0)
     tick()
     weight_grad(refs.gath_b, d_hidden, data, inner, refs.w_up.shape[0])
-    begin(at, 0)
+    begin(at, 0, 1)
     tick()
     trade.finish()
     leave_back(
@@ -1252,7 +1267,7 @@
     weight_grad(d_mixed, refs.gath_a, data, 0, used)
     tick()
     weight_grad(refs.mixture, gath, data, used, used // 3)
-    begin(at, 1)
+    begin(at, 1, 0)
     tick()
     for head in range(head_count):
         total = None
@@ -1390,7 +1405,7 @@
     pl.semaphore_wait(barrier, greeted)
     ticker = Ticker(ring)
 
-    def begin(at, kind):
+    def begin(at, kind, sub):
         if not ring:
             return
         leaf = (
@@ -1398,8 +1413,7 @@
             (refs.data_t, refs.got_t, refs.ring_send_t, refs.ring_recv_t),
         )[kind]
         streams = ring.streams(tuple(ref.at[at] for ref in leaf))
-        for first in range(0, len(streams), 2):
-            ticker.add(streams[first : first + 2])
+        ticker.add(streams[2 * sub : 2 * sub + 2])
 
     refs.grad[...] = refs.grad_in[...]
     refs.w_out[refs.w_out_all.shape[1] :] = jnp.zeros_like(refs.w_out[refs.w_out_all.shape[1] :])
@@ -1599,12 +1613,12 @@
 
     def rows(self, stream, step):
         (data, got, _, _), way, sub = stream
-        subs, piece = got.shape[1], got.shape[3]
+        piece = got.shape[3]
         if way == 0:
             chunk = (self.place + 3 * self.count - step) % self.count
         else:
             chunk = (self.place + step) % self.count
-        first = ((way * self.count + chunk) * subs + sub) * piece
+        first = ((sub * 2 + way) * self.count + chunk) * piece
         return pl.ds(pl.multiple_of(first, piece), piece)
 
     def copy(self, stream, step, gather):

time: 304 us -> 300 us (0.987)
  Pallas kernels: 291 us -> 287 us
    pallas_call x1, Pallas kernels: 84.5 us -> 81.4 us  [run_forward(): pl.pallas_call(functools.partial(forward_body, layers, head_count), name=...]
where the time goes in v1:
time: 300 us
  Pallas kernels  287 us (96%)
  local copies, waits for them, and re-layouts  7.53 us (3%)
  other arithmetic  4.27 us (1%)
    pallas_call x1, Pallas kernels, run_backward(): pl.pallas_call(functools.partial(backward_body, layers, head_count, count...  196 us
    pallas_call x1, Pallas kernels, run_forward(): pl.pallas_call(functools.partial(forward_body, layers, head_count), name=...  81.4 us
    pallas_call x1, Pallas kernels, run_widen(): pl.pallas_call(functools.partial(widen_body, wide), name='widen', grid=(s...  9.29 us

profile of v1, /device:TPU:0, one launch (start us, length us, event | category | flops | bytes accessed | tf_op | source)
XLA Modules:
  0.0 299.6 jit_solution(17975770101627024026)
XLA Ops:
  0.6 1.3 copy.37.all_refs_0_.lengths
  1.9 0.7 copy.33
  2.7 0.7 pad_convert_fusion.all_refs_5_
  3.4 1.6 pad.12
  5.0 2.4 copy.35.all_refs_11_.all_refs_15_
  7.4 81.4 %forward.1 = (bf16[2,4,256,768]{3,2,1,0:T(8,128)(2,1)}, bf16[2,4,256,768]{3,2,1,0:T(8,128)(2,1)}, bf16[2,4,3,256,256]{4,3,2,1,0:T(8,128)(2,1)}, bf16[2,4,256,256...) custom-call(s32[4,2]{1,0:T(4,128)} %copy.37.all_refs_0_.lengths, ...), custom_call_target="tpu_custom_call" | custom-call | tf_op jit(solution)/shard_map/forward/pallas_call | solution.py:750
  88.8 196.3 %backward.1 = (f32[256,768]{1,0:T(8,128)}, f32[256,768]{1,0:T(8,128)}, bf16[2,576,768]{2,1,0:T(8,128)(2,1)}, bf16[2,192,768]{2,1,0:T(8,128)(2,1)}, bf16[2,768,76...) custom-call(f32[256,768]{1,0:T(8,128)} %get-tuple-element.48.all_refs_0_, ...), custom_call_target="tpu_custom_call" | custom-call | tf_op jit(solution)/shard_map/backward/pallas_call | solution.py:1564
  285.1 0.8 slice.3
  285.9 0.6 copy.38
  286.6 3.6 %convert_bitcast_fusion = f32[2,768,3,192]{1,3,2,0:T(8,128)} fusion(bf16[2,3,192,768]{3,2,1,0:T(8,128)(2,1)} %bitcast.8), kind=kLoop, calls=%fused_computation | loop fusion | flops 884736 | bytes 5308416 | tf_op jit(solution)/shard_map/transpose | solution.py:1859
  290.1 9.3 %widen.1 = (bf16[256,768]{1,0:T(8,128)(2,1)}, f32[256,768]{1,0:T(8,128)}, f32[2,192,768]{2,1,0:T(8,128)}, f32[2,768,768]{2,1,0:T(8,128)}, f32[2,768,768]{2,1,0:T...) custom-call(s32[4,2]{1,0:T(4,128)} %copy.37.all_refs_0_.lengths, ...), custom_call_target="tpu_custom_call" | custom-call | tf_op jit(solution)/shard_map/widen/pallas_call | solution.py:1723
  (2 shorter events, 0.0 us)

commit v2 on v1

--- a/solution.py
+++ b/solution.py
@@ -347,18 +347,18 @@
     gath_b: object
     slope: object
     active: object
+    normal_a: object
+    branch_a: object
+    normal_b: object
+    branch_b: object
+    inverse: object
+    spots: object
+    turned: object
 
 
 class ForwardOutputs(NamedTuple):
     gath_z_out: object
-    spots: object
-    turned: object
     grad: object
-    normal_a: object
-    normal_b: object
-    inverse: object
-    branch_a: object
-    branch_b: object
     stream: object
 
 
@@ -431,7 +431,9 @@
     def keep(number, at):
         source = getattr(refs, ForwardKept._fields[number])
         target = getattr(refs, kept_outs[number])
-        return pltpu.make_async_copy(source.at[at], target.at[at], refs.out_sems.at[number, at])
+        if number < 12:
+            source, target = source.at[at], target.at[at]
+        return pltpu.make_async_copy(source, target, refs.out_sems.at[number, at])
 
     def layer(at, carry):
         trade = Exchange(group, 0, refs.gath_a.at[at], part, got, refs.summed)
@@ -479,6 +481,8 @@
                 refs.turned,
                 refs.same,
             )
+            keep(12, 0).start()
+            keep(13, 0).start()
             for step in loads[1:]:
                 step.wait()
 
@@ -581,6 +585,8 @@
             refs.inverse[at, 1, span] = jnp.broadcast_to(inv, (CHUNK, 128))
 
         each_chunk(rows, between)
+        for number in (7, 8, 9, 11):
+            keep(number, at).start()
 
         @pl.when(at < last)
         def _():
@@ -667,6 +673,7 @@
                 stream[span] = stream[span] + refs.layer_scale[at, 1:2] * branch
 
             each_chunk(rows, after)
+            keep(10, at).start()
             trade_b.drain_gather()
             trade_b.drain_sum()
 
@@ -690,9 +697,11 @@
         refs.gath_b.at[last, 0], refs.gath_b_kept.at[last, 0], refs.out_sems.at[4, last]
     ).wait()
     for at in range(layers):
-        for number in range(len(ForwardKept._fields)):
-            if at < last or number < 4:
+        for number in range(12):
+            if at < last or number not in (4, 5, 6, 10):
                 keep(number, at).wait()
+    keep(12, 0).wait()
+    keep(13, 0).wait()
     leave.wait()
 
 
@@ -725,9 +734,9 @@
         )
     ]
     own = full(rows, width)
-    by_layer = full(layers, rows, width)
-    near = [low(4, SPAN, rows), low(4, rows, SPAN), own, by_layer, by_layer]
-    near += [full(layers, 2, rows, 128), by_layer, by_layer, own]
+    kept += [full(layers, rows, width)] * 4 + [full(layers, 2, rows, 128)]
+    kept += [low(4, SPAN, rows), low(4, rows, SPAN)]
+    near = [own, own]
     scratch = [
         *kept,
         low(4, rows, width),
@@ -850,9 +859,9 @@
         self.ring = ring
         self.under_way = []
 
-    def add(self, streams):
+    def add(self, streams, done):
         self.ring.start(streams)
-        self.under_way.append([streams, 0])
+        self.under_way.append([streams, 0, done])
 
     def tick(self):
         if self.under_way:
@@ -860,7 +869,7 @@
 
     def one(self):
         ring = self.ring
-        streams, step = self.under_way.pop(0)
+        streams, step, done = self.under_way.pop(0)
         turn = ring.count - 1
         for stream in streams:
             if step < turn:
@@ -871,9 +880,10 @@
             if step + 1 < ring.steps:
                 ring.copy(stream, step + 1, step + 1 >= turn).start()
         if step + 1 < ring.steps:
-            self.under_way.append([streams, step + 1])
+            self.under_way.append([streams, step + 1, done])
         else:
             ring.drain(streams)
+            done()
 
     def alike(self, step):
         turn = self.ring.count - 1
@@ -883,15 +893,15 @@
         ring = self.ring
         turn = ring.count - 1
         while self.under_way:
-            run = min(self.alike(step) for _, step in self.under_way)
+            run = min(self.alike(step) for _, step, _ in self.under_way)
             if run < 2:
                 for _ in range(len(self.under_way)):
                     self.one()
                 continue
-            rings = list(self.under_way)
+            rings = [tuple(leaf) for leaf in self.under_way]
 
             def body(number, carry):
-                for streams, start in rings:
+                for streams, start, _ in rings:
                     step = start + number
                     for stream in streams:
                         if start < turn:
@@ -955,6 +965,8 @@
             (refs.gath_z, refs.gath_m),
             (refs.normal_b_all.at[at], refs.normal_b),
             (refs.inverse_all.at[at, 1], refs.inverse_b),
+            (refs.spots_all, refs.spots),
+            (refs.turned_all, refs.turned),
         ),
         refs.load_sems.at[0],
     )
@@ -1312,8 +1324,8 @@
     w_out_all: object
     w_up_all: object
     w_down_all: object
-    spots: object
-    turned: object
+    spots_all: object
+    turned_all: object
     up_bias: object
     ln_gain: object
     layer_scale: object
@@ -1331,6 +1343,8 @@
 
 
 class BackScratch(NamedTuple):
+    spots: object
+    turned: object
     branch_a: object
     branch_b: object
     normal_a: object
@@ -1404,16 +1418,34 @@
         greeted += 2
     pl.semaphore_wait(barrier, greeted)
     ticker = Ticker(ring)
+    used = refs.d_qkv.shape[1]
+    leaves = []
+
+    def leave(at, kind, sub):
+        pairs = (
+            ((refs.data_m, 0, refs.d_down),),
+            ((refs.data_m, refs.d_down.shape[1], refs.d_up),),
+            ((refs.data_t, 0, refs.d_qkv), (refs.data_t, used, refs.d_out)),
+        )[2 * kind + sub]
+        for source, first, target in pairs:
+            step = pltpu.make_async_copy(
+                source.at[at, pl.ds(first, target.shape[1])],
+                target.at[at],
+                refs.out_sems.at[len(leaves)],
+            )
+            step.start()
+            leaves.append(step)
 
     def begin(at, kind, sub):
         if not ring:
+            leave(at, kind, sub)
             return
         leaf = (
             (refs.data_m, refs.got_m, refs.ring_send_m, refs.ring_recv_m),
             (refs.data_t, refs.got_t, refs.ring_send_t, refs.ring_recv_t),
         )[kind]
         streams = ring.streams(tuple(ref.at[at] for ref in leaf))
-        ticker.add(streams[2 * sub : 2 * sub + 2])
+        ticker.add(streams[2 * sub : 2 * sub + 2], lambda: leave(at, kind, sub))
 
     refs.grad[...] = refs.grad_in[...]
     refs.w_out[refs.w_out_all.shape[1] :] = jnp.zeros_like(refs.w_out[refs.w_out_all.shape[1] :])
@@ -1469,35 +1501,16 @@
         (slice(at * SMALL_ROWS, (at + 1) * SMALL_ROWS), slice(at * 128, (at + 1) * 128))
         for at in range(width // 128)
     ]
-    used = refs.d_qkv.shape[1]
-    leaves = []
-
-    def leave(at):
-        for source, first, target in (
-            (refs.data_m, 0, refs.d_down),
-            (refs.data_m, refs.d_down.shape[1], refs.d_up),
-            (refs.data_t, 0, refs.d_qkv),
-            (refs.data_t, used, refs.d_out),
-        ):
-            step = pltpu.make_async_copy(
-                source.at[at, pl.ds(first, target.shape[1])],
-                target.at[at],
-                refs.out_sems.at[len(leaves)],
-            )
-            step.start()
-            leaves.append(step)
-
     if ring:
         small = refs.small
         small[...] = jnp.zeros_like(small)
         for rows_at, lanes in cuts:
             small[rows_at] = lines[:, lanes]
         ticker.add(
-            ring.streams((small, refs.got_small, refs.ring_send_s, refs.ring_recv_s))
+            ring.streams((small, refs.got_small, refs.ring_send_s, refs.ring_recv_s)),
+            lambda: None,
         )
         ticker.finish()
-    for at in reversed(range(layers)):
-        leave(at)
     second.wait_send()
     if ring:
         for rows_at, lanes in cuts:
@@ -1540,7 +1553,8 @@
     small_rows = -(-SMALL_ROWS * (width // 128) // (16 * ring_count)) * 16 * ring_count
     exchanges = (2 + 2 * layers) * Exchange.COPIES + 2
     scratch = (
-        [own] * 6
+        [low(4, SPAN, rows), low(4, rows, SPAN)]
+        + [own] * 6
         + [wide_rows(rows, 128)] * 2
         + [low(4, rows, wide), four, square, four, four, four, four, four, four]
         + [low(width, 3 * wide), low(wide, width), low(width, inner), low(inner, width)]
@@ -1573,7 +1587,7 @@
             jax.ShapeDtypeStruct((layers, inner, width), BF16),
             jax.ShapeDtypeStruct((SMALL_ROWS, width), F32),
         ],
-        in_specs=[in_vmem] * 2 + [in_hbm] * 17 + [in_vmem] * 6,
+        in_specs=[in_vmem] * 2 + [in_hbm] * 19 + [in_vmem] * 4,
         out_specs=[in_vmem] * 2 + [in_hbm] * 4 + [in_vmem],
         scratch_shapes=scratch,
         compiler_params=pltpu.CompilerParams(
@@ -1798,15 +1812,15 @@
         gath_b,
         slope,
         active,
-        gath_z,
+        normal_a,
+        branch_a,
+        normal_b,
+        branch_b,
+        inverse,
         spots,
         turned,
+        gath_z,
         gradient,
-        normal_a,
-        normal_b,
-        inverse,
-        branch_a,
-        branch_b,
         middle,
     ) = run_forward(
         lengths,

time: 300 us -> 296 us (0.987)
  Pallas kernels: 287 us -> 283 us
where the time goes in v2:
time: 296 us; the launch traced here: 295 us
  Pallas kernels  283 us (96%)
  local copies, waits for them, and re-layouts  7.53 us (3%)
  other arithmetic  4.27 us (1%)
    pallas_call x1, Pallas kernels, run_backward(): pl.pallas_call(functools.partial(backward_body, layers, head_count, count...  195 us
    pallas_call x1, Pallas kernels, run_forward(): pl.pallas_call(functools.partial(forward_body, layers, head_count), name=...  78.9 us
    pallas_call x1, Pallas kernels, run_widen(): pl.pallas_call(functools.partial(widen_body, wide), name='widen', grid=(s...  9.29 us

profile of v2, /device:TPU:0, one launch (start us, length us, event | category | flops | bytes accessed | tf_op | source)
XLA Modules:
  0.0 295.5 jit_solution(8987566467979048266)
XLA Ops:
  0.6 1.3 copy.37.all_refs_0_.lengths
  1.9 0.7 copy.33
  2.7 0.7 pad_convert_fusion.all_refs_5_
  3.4 1.6 pad.12
  5.0 2.4 copy.35.all_refs_11_.all_refs_15_
  7.4 78.9 %forward.1 = (bf16[2,4,256,768]{3,2,1,0:T(8,128)(2,1)}, bf16[2,4,256,768]{3,2,1,0:T(8,128)(2,1)}, bf16[2,4,3,256,256]{4,3,2,1,0:T(8,128)(2,1)}, bf16[2,4,256,256...) custom-call(s32[4,2]{1,0:T(4,128)} %copy.37.all_refs_0_.lengths, ...), custom_call_target="tpu_custom_call" | custom-call | tf_op jit(solution)/shard_map/forward/pallas_call | solution.py:759
  86.3 194.6 %backward.1 = (f32[256,768]{1,0:T(8,128)}, f32[256,768]{1,0:T(8,128)}, bf16[2,576,768]{2,1,0:T(8,128)(2,1)}, bf16[2,192,768]{2,1,0:T(8,128)(2,1)}, bf16[2,768,76...) custom-call(f32[256,768]{1,0:T(8,128)} %get-tuple-element.48.all_refs_0_, ...), custom_call_target="tpu_custom_call" | custom-call | tf_op jit(solution)/shard_map/backward/pallas_call | solution.py:1578
  281.0 0.8 slice.3
  281.8 0.6 copy.38
  282.4 3.6 %convert_bitcast_fusion = f32[2,768,3,192]{1,3,2,0:T(8,128)} fusion(bf16[2,3,192,768]{3,2,1,0:T(8,128)(2,1)} %bitcast.8), kind=kLoop, calls=%fused_computation | loop fusion | flops 884736 | bytes 5308416 | tf_op jit(solution)/shard_map/transpose | solution.py:1873
  286.0 9.3 %widen.1 = (bf16[256,768]{1,0:T(8,128)(2,1)}, f32[256,768]{1,0:T(8,128)}, f32[2,192,768]{2,1,0:T(8,128)}, f32[2,768,768]{2,1,0:T(8,128)}, f32[2,768,768]{2,1,0:T...) custom-call(s32[4,2]{1,0:T(4,128)} %copy.37.all_refs_0_.lengths, ...), custom_call_target="tpu_custom_call" | custom-call | tf_op jit(solution)/shard_map/widen/pallas_call | solution.py:1737
  (2 shorter events, 0.0 us)

commit v3 on v2

--- a/solution.py
+++ b/solution.py
@@ -1717,7 +1717,7 @@
 def run_widen(lengths, stream, gradient, d_out, d_up, d_down, small, wide, used):
     rows, width = stream.shape
     layers = d_out.shape[0]
-    parts = 4
+    parts = 2
     steps = layers * parts
 
     def rows_of(total):

time: 296 us -> 295 us (level)
  no operation moved by 1% of the time
where the time goes in v3:
time: 295 us; the launch traced here: 294 us
  Pallas kernels  282 us (96%)
  local copies, waits for them, and re-layouts  7.53 us (3%)
  other arithmetic  4.27 us (1%)
    pallas_call x1, Pallas kernels, run_backward(): pl.pallas_call(functools.partial(backward_body, layers, head_count, count...  195 us
    pallas_call x1, Pallas kernels, run_forward(): pl.pallas_call(functools.partial(forward_body, layers, head_count), name=...  78.9 us
    pallas_call x1, Pallas kernels, run_widen(): pl.pallas_call(functools.partial(widen_body, wide), name='widen', grid=(s...  8.12 us

profile of v3, /device:TPU:0, one launch (start us, length us, event | category | flops | bytes accessed | tf_op | source)
XLA Modules:
  0.0 294.3 jit_solution(16824261149097207815)
XLA Ops:
  0.6 1.3 copy.37.all_refs_0_.lengths
  1.9 0.7 copy.33
  2.7 0.7 pad_convert_fusion.all_refs_5_
  3.4 1.6 pad.12
  5.0 2.4 copy.35.all_refs_11_.all_refs_15_
  7.4 78.9 %forward.1 = (bf16[2,4,256,768]{3,2,1,0:T(8,128)(2,1)}, bf16[2,4,256,768]{3,2,1,0:T(8,128)(2,1)}, bf16[2,4,3,256,256]{4,3,2,1,0:T(8,128)(2,1)}, bf16[2,4,256,256...) custom-call(s32[4,2]{1,0:T(4,128)} %copy.37.all_refs_0_.lengths, ...), custom_call_target="tpu_custom_call" | custom-call | tf_op jit(solution)/shard_map/forward/pallas_call | solution.py:759
  86.3 194.6 %backward.1 = (f32[256,768]{1,0:T(8,128)}, f32[256,768]{1,0:T(8,128)}, bf16[2,576,768]{2,1,0:T(8,128)(2,1)}, bf16[2,192,768]{2,1,0:T(8,128)(2,1)}, bf16[2,768,76...) custom-call(f32[256,768]{1,0:T(8,128)} %get-tuple-element.48.all_refs_0_, ...), custom_call_target="tpu_custom_call" | custom-call | tf_op jit(solution)/shard_map/backward/pallas_call | solution.py:1578
  281.0 0.8 slice.3
  281.8 0.6 copy.38
  282.4 3.6 %convert_bitcast_fusion = f32[2,768,3,192]{1,3,2,0:T(8,128)} fusion(bf16[2,3,192,768]{3,2,1,0:T(8,128)(2,1)} %bitcast.8), kind=kLoop, calls=%fused_computation | loop fusion | flops 884736 | bytes 5308416 | tf_op jit(solution)/shard_map/transpose | solution.py:1873
  286.0 8.1 %widen.1 = (bf16[256,768]{1,0:T(8,128)(2,1)}, f32[256,768]{1,0:T(8,128)}, f32[2,192,768]{2,1,0:T(8,128)}, f32[2,768,768]{2,1,0:T(8,128)}, f32[2,768,768]{2,1,0:T...) custom-call(s32[4,2]{1,0:T(4,128)} %copy.37.all_refs_0_.lengths, ...), custom_call_target="tpu_custom_call" | custom-call | tf_op jit(solution)/shard_map/widen/pallas_call | solution.py:1737
  (2 shorter events, 0.0 us)

commit v4 on v3

--- a/solution.py
+++ b/solution.py
@@ -602,13 +602,13 @@
                 refs.hidden[...] = dot(refs.gath_b[at, slot], refs.w_up[at]) + refs.up_bias[at]
 
                 def act(place, carry):
-                    span = pl.ds(pl.multiple_of(place * 16, 16), 16)
+                    span = pl.ds(pl.multiple_of(place * CHUNK, CHUNK), CHUNK)
                     high, incline = gelu_parts(refs.hidden[span])
                     refs.active[at, slot, span] = high.astype(BF16)
                     refs.slope[at, slot, span] = incline.astype(BF16)
                     return carry
 
-                lax.fori_loop(0, rows // 16, act, 0)
+                lax.fori_loop(0, rows // CHUNK, act, 0)
 
             def lower(slot, first, count):
                 return dot(refs.active[at, slot, pl.ds(first, count)], refs.w_down[at])
@@ -981,7 +981,7 @@
         refs.hidden_f[...] = dot(refs.gath_m[slot], refs.w_down[...], 1, 1)
 
         def act(place, carry):
-            span = pl.ds(pl.multiple_of(place * 16, 16), 16)
+            span = pl.ds(pl.multiple_of(place * CHUNK, CHUNK), CHUNK)
             high, incline = gelu_parts(refs.hidden[span])
             refs.active[slot, span] = high.astype(BF16)
             back = (refs.hidden_f[span] * incline).astype(BF16)
@@ -989,7 +989,7 @@
             refs.up_total[...] += fold(back.astype(F32))
             return carry
 
-        lax.fori_loop(0, rows // 16, act, 0)
+        lax.fori_loop(0, rows // CHUNK, act, 0)
 
     refs.up_total[...] = jnp.zeros_like(refs.up_total)
 

time: 295 us -> 294 us (level)
  no operation moved by 1% of the time
where the time goes in v4:
time: 294 us
  Pallas kernels  281 us (96%)
  local copies, waits for them, and re-layouts  7.53 us (3%)
  other arithmetic  4.27 us (1%)
    pallas_call x1, Pallas kernels, run_backward(): pl.pallas_call(functools.partial(backward_body, layers, head_count, count...  194 us
    pallas_call x1, Pallas kernels, run_forward(): pl.pallas_call(functools.partial(forward_body, layers, head_count), name=...  78.8 us
    pallas_call x1, Pallas kernels, run_widen(): pl.pallas_call(functools.partial(widen_body, wide), name='widen', grid=(s...  8.12 us

profile of v4, /device:TPU:0, one launch (start us, length us, event | category | flops | bytes accessed | tf_op | source)
XLA Modules:
  0.0 293.9 jit_solution(18091089931163631108)
XLA Ops:
  0.6 1.3 copy.37.all_refs_0_.lengths
  1.9 0.7 copy.33
  2.7 0.7 pad_convert_fusion.all_refs_5_
  3.4 1.6 pad.12
  5.0 2.4 copy.35.all_refs_11_.all_refs_15_
  7.4 78.8 %forward.1 = (bf16[2,4,256,768]{3,2,1,0:T(8,128)(2,1)}, bf16[2,4,256,768]{3,2,1,0:T(8,128)(2,1)}, bf16[2,4,3,256,256]{4,3,2,1,0:T(8,128)(2,1)}, bf16[2,4,256,256...) custom-call(s32[4,2]{1,0:T(4,128)} %copy.37.all_refs_0_.lengths, ...), custom_call_target="tpu_custom_call" | custom-call | tf_op jit(solution)/shard_map/forward/pallas_call | solution.py:759
  86.2 194.4 %backward.1 = (f32[256,768]{1,0:T(8,128)}, f32[256,768]{1,0:T(8,128)}, bf16[2,576,768]{2,1,0:T(8,128)(2,1)}, bf16[2,192,768]{2,1,0:T(8,128)(2,1)}, bf16[2,768,76...) custom-call(f32[256,768]{1,0:T(8,128)} %get-tuple-element.48.all_refs_0_, ...), custom_call_target="tpu_custom_call" | custom-call | tf_op jit(solution)/shard_map/backward/pallas_call | solution.py:1578
  280.6 0.8 slice.3
  281.5 0.6 copy.38
  282.1 3.6 %convert_bitcast_fusion = f32[2,768,3,192]{1,3,2,0:T(8,128)} fusion(bf16[2,3,192,768]{3,2,1,0:T(8,128)(2,1)} %bitcast.8), kind=kLoop, calls=%fused_computation | loop fusion | flops 884736 | bytes 5308416 | tf_op jit(solution)/shard_map/transpose | solution.py:1873
  285.7 8.1 %widen.1 = (bf16[256,768]{1,0:T(8,128)(2,1)}, f32[256,768]{1,0:T(8,128)}, f32[2,192,768]{2,1,0:T(8,128)}, f32[2,768,768]{2,1,0:T(8,128)}, f32[2,768,768]{2,1,0:T...) custom-call(s32[4,2]{1,0:T(4,128)} %copy.37.all_refs_0_.lengths, ...), custom_call_target="tpu_custom_call" | custom-call | tf_op jit(solution)/shard_map/widen/pallas_call | solution.py:1737
  (2 shorter events, 0.0 us)
